TPU v7x, 32 devices: a whole 2x2x4 slice. The times are simulated.
32 devices in a mesh: band: 4 (over y, core), shard: 8 (over z, x).
Axes of the slice: x: 2, y: 2, z: 4, core: 2. Of those that a mesh axis runs over, the one named last changes fastest.
Arguments:
- activations: bfloat16 [512, 2304], P('shard'), may hold values from -6 to 6
- encoder: bfloat16 [2304, 16384], P(None, ('band', 'shard')), may hold values from -0.125 to 0.125
- encoder_bias: float32 [16384], P(('band', 'shard')), may hold values from -1 to -0.25
- decoder: bfloat16 [16384, 2304], P(('band', 'shard')), may hold values from -0.125 to 0.125
Outputs:
- losses: float32 [4], replicated
- encoder_grad: bfloat16 [2304, 16384], P(None, ('band', 'shard'))
- decoder_grad: bfloat16 [16384, 2304], P(('band', 'shard'))
All inputs are finite; a program needn't handle non-finite values.
Results may differ from a plain program's by a relative error of at most 0.006.
Values may be sent and summed in bfloat16 or wider, within the bound.
A program may use at most 128 MiB of HBM per device.

v0:
```python
import jax
import jax.numpy as jnp
from jax import lax
from jax.sharding import PartitionSpec as P


def on_device(activations, encoder, encoder_bias, decoder):
    band_count = lax.axis_size("band")
    local_count = activations.shape[0]
    divisor = local_count * lax.axis_size("shard") * activations.shape[1]
    gathered = lax.all_gather(activations, "shard", axis=0, tiled=True)
    preact = jnp.dot(gathered, encoder, preferred_element_type=jnp.float32) + encoder_bias
    linear = jnp.maximum(preact, 0.0)
    active = (linear * linear).astype(jnp.bfloat16)
    act_rows = active
    band_part = lax.psum_scatter(
        jnp.dot(act_rows, decoder, preferred_element_type=jnp.float32),
        "shard",
        scatter_dimension=0,
        tiled=True,
    )
    local_rows = activations.astype(jnp.float32)
    stacked = lax.all_gather(band_part[None], "band", axis=0, tiled=True)
    prefix_recon = jnp.cumsum(stacked, axis=0)
    errors_all = local_rows[None] - prefix_recon
    losses = lax.psum(jnp.sum(errors_all * errors_all, axis=(1, 2)), "shard") / divisor
    tail_sums = jnp.flip(jnp.cumsum(jnp.flip(errors_all, 0), axis=0), 0)
    suffix = lax.dynamic_index_in_dim(tail_sums, lax.axis_index("band"), 0, keepdims=False)
    upstream = (-suffix / band_count).astype(jnp.bfloat16)
    shard_rows = lax.all_gather(upstream, "shard", axis=0, tiled=True)
    act_block = jnp.einsum("rd,ld->rl", shard_rows, decoder, preferred_element_type=jnp.float32)
    act_grads = act_block
    act_rows = active
    dec_grads = jnp.einsum("rl,rd->ld", act_rows, shard_rows, preferred_element_type=jnp.float32)
    act_grads, dec_grads = (act_grads, dec_grads)
    pre_grads = (2.0 * linear * act_grads).astype(jnp.bfloat16)
    encoder_grad = jnp.einsum(
        "rd,rl->dl", gathered, pre_grads, preferred_element_type=jnp.float32
    ).astype(jnp.bfloat16)
    return (losses, encoder_grad, dec_grads.astype(jnp.bfloat16))


def solution(mesh):
    return jax.shard_map(
        on_device,
        mesh=mesh,
        in_specs=(
            P("shard", None),
            P(None, ("band", "shard")),
            P(("band", "shard")),
            P(("band", "shard"), None),
        ),
        out_specs=(P(), P(None, ("band", "shard")), P(("band", "shard"), None)),
        check_vma=False,
    )
```

profile of v0, /device:TPU:0, one launch (start us, length us, event | category | flops | bytes accessed | tf_op | source)
XLA Modules:
  0.0 282.0 jit_solution(15848394978107136269)
XLA Ops:
  7.2 0.0 copy-start
  7.2 0.0 all-gather.6.cloned.1.call-start
  7.2 0.7 all-gather.6.cloned.1.call-update
  7.9 0.0 reduce-scatter.2.cloned.1.call-start
  8.0 56.8 %all-gather.6.cloned.1.call-done = bf16[512,2304]{1,0:T(8,128)(2,1)} async-done(((bf16[64,2304]{1,0:T(8,128)(2,1)}), bf16[512,2304]{1,0:T(8,128)(2,1)}) %all-gather.6.cloned.1.call-update) | async-done | bytes 2359312 | tf_op jit(solution)/shard_map/all_gather | solution.py:11
  64.7 3.8 %fusion.7 = f32[512,512]{1,0:T(8,128)S(1)} fusion(bf16[512,2304]{1,0:T(8,128)(2,1)} %all-gather.6.cloned.1.call-done, bf16[2304,512]{1,0:T(8,128)(2,1)} %param.5, f32[512]{0:T(512)} %param.6), kind=kOutput, calls=%fused_computation.10 | convolution fusion | flops 1208483840 | bytes 5769216 | tf_op jit(solution)/shard_map/dot_general | solution.py:12
  68.5 0.0 copy-start.2
  68.5 1.0 copy-done.2
  69.5 0.0 copy-done
  69.5 3.5 %fusion.14 = f32[512,2304]{1,0:T(8,128)} fusion(bf16[512,2304]{1,0:T(8,128)(2,1)S(1)} %copy-done, f32[512,512]{1,0:T(8,128)S(1)} %fusion.7), kind=kOutput, calls=%fused_computation.15 | convolution fusion | flops 1208483840 | bytes 8126464 | tf_op jit(solution)/shard_map/dot_general | solution.py:17
  73.0 0.0 copy-start.1
  73.0 0.0 reduce-scatter.2.cloned.1.call-update
  73.0 0.0 all-gather.8.cloned.1.call-start
  73.1 94.3 %reduce-scatter.2.cloned.1.call-done = f32[64,2304]{1,0:T(8,128)} async-done(((f32[512,2304]{1,0:T(8,128)}), f32[64,2304]{1,0:T(8,128)}) %reduce-scatter.2.cloned.1.call-update) | async-done | bytes 589840 | tf_op jit(solution)/shard_map/reduce_scatter | solution.py:16
  167.4 0.0 all-gather.8.cloned.1.call-update
  167.4 0.0 all-gather.10.cloned.1.call-start
  167.4 0.0 copy-done.1
  167.5 25.2 %all-gather.8.cloned.1.call-done = f32[256,2304]{1,0:T(8,128)} async-done(((f32[64,2304]{1,0:T(8,128)}), f32[256,2304]{1,0:T(8,128)}) %all-gather.8.cloned.1.call-update) | async-done | bytes 2359312 | tf_op jit(solution)/shard_map/all_gather | solution.py:23
  192.7 3.5 %multiply_reduce_fusion = (f32[4]{0:T(128)S(1)}, f32[4,64,2304]{2,1,0:T(8,128)}) fusion(f32[4,64,2304]{2,1,0:T(8,128)} %bitcast.21, f32[64,2304]{1,0:T(8,128)S(1)} %convert_element_type.24), kind=kOutput, calls=%fused_computation.7 | output fusion | flops 3538940 | bytes 5308432 | tf_op jit(solution)/shard_map/jit(cumsum)/reduce_window_sum | solution.py:24
  196.1 3.3 %rev.7 = f32[4,64,2304]{2,1,0:T(8,128)} reverse(f32[4,64,2304]{2,1,0:T(8,128)} %get-tuple-element.7), dimensions={0} | reverse | bytes 4718592 | tf_op jit(solution)/shard_map/jit(_flip)/rev | solution.py:27
  199.4 3.2 %fusion.16 = f32[4,64,2304]{2,1,0:T(8,128)} fusion(f32[4,64,2304]{2,1,0:T(8,128)} %rev.7), kind=kOutput, calls=%fused_computation.18 | output fusion | flops 1769472 | bytes 4718592 | tf_op jit(solution)/shard_map/jit(cumsum)/reduce_window_sum | solution.py:27
  202.7 0.0 copy-start.3
  202.7 3.4 %rev.8 = f32[4,64,2304]{2,1,0:T(8,128)} reverse(f32[4,64,2304]{2,1,0:T(8,128)} %fusion.16), dimensions={0} | reverse | bytes 4718592 | tf_op jit(solution)/shard_map/jit(_flip)/rev | solution.py:27
  206.0 1.8 multiply_convert_fusion.1
  207.9 0.0 all-gather.10.cloned.1.call-update
  207.9 21.5 %psum.7 = f32[4]{0:T(128)S(1)} all-reduce(f32[4]{0:T(128)S(1)} %get-tuple-element.6), channel_id=1, replica_groups=mesh['band'=4,'shard'=8] {'shard'}, use_global_device_ids=true, to_apply=%region_3.4 | all-reduce | flops 4 | bytes 32 | tf_op jit(solution)/shard_map/psum | solution.py:26
  229.4 0.5 broadcast_multiply_fusion
  229.9 30.0 %all-gather.10.cloned.1.call-done = bf16[1,512,2304]{2,1,0:T(8,128)(2,1)} async-done(((bf16[1,64,2304]{2,1,0:T(8,128)(2,1)}), bf16[1,512,2304]{2,1,0:T(8,128)(2,1)}) %all-gather.10.cloned.1.call-update) | async-done | bytes 2359312 | tf_op jit(solution)/shard_map/all_gather | solution.py:30
  259.9 0.0 copy-done.3
  259.9 6.7 %fusion = bf16[2304,512]{0,1:T(8,128)(2,1)} fusion(bf16[512,2304]{1,0:T(8,128)(2,1)} %all-gather.6.cloned.1.call-done, bf16[512,2304]{1,0:T(8,128)(2,1)S(1)} %copy-done, bf16[1,512,2304]{2,1,0:T(8,128)(2,1)} %all-gather.10.cloned.1.call-done, f32[512,512]{1,0:T(8,128)S(1)} %copy-done.3), kind=kOutput, calls=%fused_computation.3 | convolution fusion | flops 2417885184 | bytes 10485760 | tf_op jit(solution)/shard_map/rd,rl->dl/dot_general | solution.py:37
  266.7 4.3 %copy.7 = bf16[2304,512]{1,0:T(8,128)(2,1)} copy(bf16[2304,512]{0,1:T(8,128)(2,1)} %fusion) | data formatting | bytes 4718592
  270.9 4.5 %convolution_convert_fusion = bf16[512,2304]{1,0:T(8,128)(2,1)} fusion(bf16[1,512,2304]{2,1,0:T(8,128)(2,1)} %all-gather.10.cloned.1.call-done, f32[512,512]{1,0:T(8,128)S(1)} %copy-done.3), kind=kOutput, calls=%fused_computation | convolution fusion | flops 1209663488 | bytes 5767168 | tf_op jit(solution)/shard_map/rl,rd->ld/dot_general | solution.py:34
  (1 shorter events, 0.0 us)
Async XLA Ops:
  7.2 62.3 %copy-start = (bf16[512,2304]{1,0:T(8,128)(2,1)S(1)}, bf16[512,2304]{1,0:T(8,128)(2,1)}, u32[]{:S(2)}) copy-start(bf16[512,2304]{1,0:T(8,128)(2,1)} %param.7) | copy-start | bytes 7077892
  7.2 57.6 %all-gather.6.cloned.1.call-start = ((), (), s32[]{:S(2)}) async-start(), calls=%async_computation.1 | async-start | bytes 2654208 | tf_op jit(solution)/shard_map/all_gather | solution.py:11
  7.9 159.5 %reduce-scatter.2.cloned.1.call-start = ((), (), s32[]{:S(2)}) async-start(), calls=%async_computation.2 | async-start | bytes 5308416 | tf_op jit(solution)/shard_map/reduce_scatter | solution.py:16
  68.5 1.0 copy-start.2
  73.0 94.4 %copy-start.1 = (bf16[64,2304]{1,0:T(8,128)(2,1)S(1)}, bf16[64,2304]{1,0:T(8,128)(2,1)}, u32[]{:S(2)}) copy-start(bf16[64,2304]{1,0:T(8,128)(2,1)} %param.4) | copy-start | bytes 884740
  73.0 119.6 %all-gather.8.cloned.1.call-start = ((), (), s32[]{:S(2)}) async-start(), calls=%async_computation.3 | async-start | bytes 2949120 | tf_op jit(solution)/shard_map/all_gather | solution.py:23
  167.4 92.5 %all-gather.10.cloned.1.call-start = ((), (), s32[]{:S(2)}) async-start(), calls=%async_computation.4 | async-start | bytes 2654208 | tf_op jit(solution)/shard_map/all_gather | solution.py:30
  202.7 57.3 %copy-start.3 = (f32[512,512]{1,0:T(8,128)S(1)}, f32[512,512]{1,0:T(8,128)}, u32[]{:S(2)}) copy-start(f32[512,512]{1,0:T(8,128)} %copy-done.2) | copy-start | bytes 3145732
Sparse Core Ops, SparseCore 0:
  10.2 54.5 all-gather.5
  73.2 94.1 reduce-scatter.1
  168.9 23.6 all-gather.7
  208.0 51.8 all-gather.9
where the time goes:
time: 282 us
  waiting for transfers between devices  207 us (73%)
  blocking collectives  21.5 us (8%)
  matrix products  18.5 us (7%)
  between operations  13.8 us (5%)
  local copies, waits for them, and re-layouts  11.9 us (4%)
  other arithmetic  9.06 us (3%)
    reduce_scatter x1, waiting for transfers between devices, on_device(): lax.psum_scatter(jnp.dot(act_rows, decoder, preferred_element_type=jnp.fl...  94.3 us
    all_gather x1, waiting for transfers between devices, on_device(): gathered = lax.all_gather(activations, 'shard', axis=0, tiled=True)  56.8 us
    all_gather x1, waiting for transfers between devices, on_device(): shard_rows = lax.all_gather(upstream, 'shard', axis=0, tiled=True)  30 us
    all_gather x1, waiting for transfers between devices, on_device(): stacked = lax.all_gather(band_part[None], 'band', axis=0, tiled=True)  25.2 us
    psum x1, blocking collectives, on_device(): lax.psum(jnp.sum(errors_all * errors_all, axis=(1, 2)), 'shard') / divisor  21.5 us
    dot_general x1, matrix products, on_device(): jnp.einsum('rd,rl->dl', gathered, pre_grads, preferred_element_type=jnp.f...  6.73 us
    rev x2, local copies, waits for them, and re-layouts, on_device(): tail_sums = jnp.flip(jnp.cumsum(jnp.flip(errors_all, 0), axis=0), 0)  6.68 us
  transfers between devices with their start and end apart: 4, of which 4 were waited for; matrix products, arithmetic and copies ran while one was open for 0% of the time, Pallas kernels for 0%

commit v1 on v0

v1 whole, which is shorter than its diff:
```python
import functools

import jax
import jax.numpy as jnp
from jax import lax
from jax.experimental import pallas as pl
from jax.experimental.pallas import tpu as pltpu
from jax.sharding import PartitionSpec as P

MESH = pl.DeviceIdType.MESH
CHUNKS = 2
F32 = jnp.float32
BF16 = jnp.bfloat16


def factors(count):
    outer = next(a for a in range(1, count + 1) if count % a == 0 and a * a >= count)
    return outer, count // outer


def ring_position(index, outer, inner):
    z, x = index // inner, index % inner
    return x * outer + z + (x % 2) * (outer - 1 - 2 * z)


def ring_index(position, outer, inner):
    x, r = position // outer, position % outer
    z = r + (x % 2) * (outer - 1 - 2 * r)
    return z * inner + x


def tile_of(extent, most):
    return next(t for t in range(most, 0, -128) if extent % t == 0)


def kernel(
    n, nb,
    act_ref, act3_ref, enc_hbm, bias_ref, dec_hbm,
    gath, ups, active, pregr, loss_ref,
    enc, dec, linear, part, sendb, recvb, xsend, xrecv, usend, urecv, loss_acc, loss1s, loss1, loss2s, loss2,
    load_sem,
    ag_s, ag_r, pt_s, pt_r, rs_s, rs_r, bx_s, bx_r, bu_s, bu_r, l1_s, l1_r, l2_s, l2_r, ug_s, ug_r,
):
    rows, width = act_ref.shape
    half = rows // 2
    chunk = rows // CHUNKS
    thin = rows // nb
    latents = enc.shape[1]
    fwd, bwd = n // 2, n // 2 - 1
    outer, inner = factors(n)
    band = lax.axis_index("band")
    shard = lax.axis_index("shard")
    core = band % 2
    sign = 1 - 2 * core
    place = ring_position(shard, outer, inner)
    nxt = {"shard": ring_index((place + n + sign) % n, outer, inner)}
    prv = {"shard": ring_index((place + n - sign) % n, outer, inner)}
    mate = {"band": band + sign}
    ours = pl.multiple_of(core * half, half)

    load_enc = pltpu.make_async_copy(enc_hbm, enc, load_sem.at[0])
    load_dec = pltpu.make_async_copy(dec_hbm, dec, load_sem.at[1])
    load_enc.start()
    load_dec.start()

    barrier = pltpu.get_barrier_semaphore()
    for step in range(1, n):
        pl.semaphore_signal(barrier, inc=1, device_id={"shard": (shard + step) % n}, device_id_type=MESH)
    for step in range(1, nb):
        pl.semaphore_signal(barrier, inc=1, device_id={"band": (band + step) % nb}, device_id_type=MESH)
    pl.semaphore_wait(barrier, n - 1 + nb - 1)

    started = []

    def remote(src, dst, send, recv, device):
        return pltpu.make_async_remote_copy(
            src_ref=src, dst_ref=dst, send_sem=send, recv_sem=recv, device_id=device, device_id_type=MESH
        )

    def go(copy):
        copy.start()
        started.append(copy)
        return copy

    def held(slot):
        return gath.at[pl.ds(pl.multiple_of(slot * rows + ours, half), half), :]

    mine = act_ref.at[pl.ds(ours, half), :]

    def ag_copy(way, t):
        if way == 0:
            src = mine if t == 1 else held(n - t + 1)
            return remote(src, held(n - t), ag_s.at[0, t], ag_r.at[0, t], nxt)
        src = mine if t == 1 else held(t - 1)
        return remote(src, held(t), ag_s.at[1, t], ag_r.at[1, t], prv)

    def mate_copy(slot):
        there = n - slot
        return remote(held(slot), held(there), pt_s.at[slot], pt_r.at[there], mate)

    def preact(group):
        span = pl.ds(group * 2 * rows, 2 * rows)
        value = jnp.dot(gath[span, :], enc[...], preferred_element_type=F32) + bias_ref[...]
        value = jnp.maximum(value, 0.0)
        linear[span, :] = value
        active[span, :] = (value * value).astype(BF16)

    def ready(slot):
        return slot if slot <= bwd else n - slot

    ag = {(0, 1): go(ag_copy(0, 1)), (1, 1): go(ag_copy(1, 1))}
    gath[pl.ds(0, rows), :] = act_ref[...]
    mates = {}
    for t in range(1, fwd + 1):
        ag[0, t].wait_recv()
        if t < fwd:
            ag[0, t + 1] = go(ag_copy(0, t + 1))
        mates[n - t] = go(mate_copy(n - t))
        if t <= bwd:
            ag[1, t].wait_recv()
            if t < bwd:
                ag[1, t + 1] = go(ag_copy(1, t + 1))
            mates[t] = go(mate_copy(t))
        for group in range(n // 2):
            pair = (2 * group, 2 * group + 1)
            if max(ready(s) for s in pair) == t:
                for s in pair:
                    if s:
                        remote(held(s), held(s), pt_s.at[n - s], pt_r.at[s], mate).wait_recv()
                if t == 1:
                    load_enc.wait()
                preact(group)
    load_dec.wait()

    tile = tile_of(width, 768)

    def decode(group):
        span = pl.ds(group * 2 * rows, 2 * rows)

        def body(i, carry):
            cols = pl.ds(pl.multiple_of(i * tile, tile), tile)
            part[span, cols] = jnp.dot(active[span, :], dec[:, cols], preferred_element_type=F32)
            return carry

        lax.fori_loop(0, width // tile, body, 0)

    def need(slot):
        return n if slot == 0 else (fwd - slot + 1 if slot <= fwd else slot - fwd)

    def rs_copy(way, t, c):
        slot = fwd - t + 1 if way == 0 else fwd + t
        there = slot - 1 if way == 0 else (slot + 1 if slot + 1 < n else fwd)
        span = pl.ds(c * chunk, chunk)
        return remote(
            sendb.at[slot, span, :], recvb.at[there, span, :], rs_s.at[way, t, c], rs_r.at[way, t, c],
            nxt if way == 0 else prv,
        )

    order = sorted(range(n // 2), key=lambda g: min(need(2 * g), need(2 * g + 1)))
    first = [g for g in order if min(need(2 * g), need(2 * g + 1)) == 1]
    for group in first:
        decode(group)
    rs = {}
    for t in range(1, fwd + 1):
        for c in range(CHUNKS):
            for way in (0, 1):
                if way == 1 and t > bwd:
                    continue
                slot = fwd - t + 1 if way == 0 else fwd + t
                span = pl.ds(c * chunk, chunk)
                value = part[pl.ds(slot * rows + c * chunk, chunk), :]
                if t > 1:
                    rs[way, t - 1, c].wait_recv()
                    value = value + recvb[slot, span, :].astype(F32)
                sendb[slot, span, :] = value.astype(BF16)
                rs[way, t, c] = go(rs_copy(way, t, c))
        if t == 1:
            for group in order:
                if group not in first:
                    decode(group)
    for c in range(CHUNKS):
        span = pl.ds(c * chunk, chunk)
        rs[1, bwd, c].wait_recv()
        rs[0, fwd, c].wait_recv()
        part[span, :] = part[span, :] + recvb[0, span, :].astype(F32) + recvb[fwd, span, :].astype(F32)

    for k in range(nb):
        xsend[k] = part[pl.ds(k * thin, thin), :].astype(BF16)
    bx = [
        go(remote(xsend.at[(band + i) % nb], xrecv.at[band], bx_s.at[i], bx_r.at[i], {"band": (band + i) % nb}))
        for i in range(1, nb)
    ]
    xrecv[band] = xsend[band]
    for copy in bx:
        copy.wait_recv()

    step_cols = tile_of(width, 256)

    def errors(i, carry):
        cols = pl.ds(pl.multiple_of(i * step_cols, step_cols), step_cols)
        left = act3_ref[band, :, cols].astype(F32)
        all_errors = []
        for k in range(nb):
            left = left - xrecv[k, :, cols].astype(F32)
            all_errors.append(left)
            loss_acc[pl.ds(k, 1), cols] = jnp.sum(left * left, axis=0, keepdims=True)
        total = jnp.zeros_like(left)
        for k in reversed(range(nb)):
            total = total + all_errors[k]
            usend[k, :, cols] = (-total / nb).astype(BF16)
        return carry

    lax.fori_loop(0, width // step_cols, errors, 0)
    bu = [
        go(remote(usend.at[(band + i) % nb], urecv.at[band], bu_s.at[i], bu_r.at[i], {"band": (band + i) % nb}))
        for i in range(1, nb)
    ]
    urecv[band] = usend[band]
    loss1s[...] = jnp.broadcast_to(jnp.sum(loss_acc[...], axis=1, keepdims=True), loss1s.shape)
    l1 = [
        go(remote(loss1s, loss1.at[i], l1_s.at[i], l1_r.at[i], {"band": (band + i) % nb}))
        for i in range(1, nb)
    ]
    for copy in bu:
        copy.wait_recv()
    if thin % 16 == 0:
        for k in range(nb):
            ups[pl.ds(k * thin, thin), :] = urecv[k]
    else:
        ups[pl.ds(0, rows), :] = jnp.concatenate([urecv[k].astype(F32) for k in range(nb)], axis=0).astype(BF16)

    def ug_copy(way, t, c):
        if way == 0:
            slot, there, device = (n - t + 1) % n, n - t, nxt
        else:
            slot, there, device = t - 1, t, prv
        return remote(
            ups.at[pl.ds(slot * rows + c * chunk, chunk), :], ups.at[pl.ds(there * rows + c * chunk, chunk), :],
            ug_s.at[way, t, c], ug_r.at[way, t, c], device,
        )

    ug = {}
    for c in range(CHUNKS):
        for way in (0, 1):
            ug[way, 1, c] = go(ug_copy(way, 1, c))

    for copy in l1:
        copy.wait_recv()
    total = loss1s[...]
    for i in range(1, nb):
        total = total + loss1[i]
    loss2s[...] = total
    l2 = [
        go(remote(loss2s, loss2.at[i], l2_s.at[i], l2_r.at[i], {"shard": (shard + i) % n}))
        for i in range(1, n)
    ]

    def backward(group):
        span = pl.ds(group * 2 * rows, 2 * rows)
        grads = lax.dot_general(ups[span, :], dec[...], (((1,), (1,)), ((), ())), preferred_element_type=F32)
        pregr[span, :] = (2.0 * linear[span, :] * grads).astype(BF16)

    for t in range(1, fwd + 1):
        for c in range(CHUNKS):
            for way in (0, 1):
                last = fwd if way == 0 else bwd
                if t > last:
                    continue
                ug[way, t, c].wait_recv()
                if t < last:
                    ug[way, t + 1, c] = go(ug_copy(way, t + 1, c))
        for group in range(n // 2):
            if max(ready(2 * group), ready(2 * group + 1)) == t:
                backward(group)

    for copy in l2:
        copy.wait_recv()
    total = loss2s[...]
    for i in range(1, n):
        total = total + loss2[i]
    loss_ref[...] = total
    for copy in started:
        copy.wait_send()


def on_device(n, nb, activations, encoder, encoder_bias, decoder):
    rows, width = activations.shape
    latents = encoder.shape[1]
    every = n * rows
    thin = rows // nb
    sem = pltpu.SemaphoreType.DMA
    vmem = pl.BlockSpec(memory_space=pltpu.VMEM)
    hbm = pl.BlockSpec(memory_space=pl.ANY)
    steps = n // 2 + 1
    gathered, upstream, active, pre_grads, losses = pl.pallas_call(
        functools.partial(kernel, n, nb),
        out_shape=(
            jax.ShapeDtypeStruct((every, width), BF16),
            jax.ShapeDtypeStruct((every, width), BF16),
            jax.ShapeDtypeStruct((every, latents), BF16),
            jax.ShapeDtypeStruct((every, latents), BF16),
            jax.ShapeDtypeStruct((nb, 128), F32),
        ),
        in_specs=[vmem, vmem, hbm, vmem, hbm],
        out_specs=[vmem] * 5,
        scratch_shapes=[
            pltpu.VMEM((width, latents), BF16),
            pltpu.VMEM((latents, width), BF16),
            pltpu.VMEM((every, latents), F32),
            pltpu.VMEM((every, width), F32),
            pltpu.VMEM((n, rows, width), BF16),
            pltpu.VMEM((n, rows, width), BF16),
            pltpu.VMEM((nb, thin, width), BF16),
            pltpu.VMEM((nb, thin, width), BF16),
            pltpu.VMEM((nb, thin, width), BF16),
            pltpu.VMEM((nb, thin, width), BF16),
            pltpu.VMEM((nb, width), F32),
            pltpu.VMEM((nb, 128), F32),
            pltpu.VMEM((nb, nb, 128), F32),
            pltpu.VMEM((nb, 128), F32),
            pltpu.VMEM((n, nb, 128), F32),
            sem((2,)),
            sem((2, steps)), sem((2, steps)),
            sem((n,)), sem((n,)),
            sem((2, steps, CHUNKS)), sem((2, steps, CHUNKS)),
            sem((nb,)), sem((nb,)),
            sem((nb,)), sem((nb,)),
            sem((nb,)), sem((nb,)),
            sem((n,)), sem((n,)),
            sem((2, steps, CHUNKS)), sem((2, steps, CHUNKS)),
        ],
        compiler_params=pltpu.CompilerParams(
            collective_id=0, has_side_effects=True, vmem_limit_bytes=60 * 1024 * 1024
        ),
    )(activations, activations.reshape(nb, thin, width), encoder, encoder_bias.reshape(1, latents), decoder)
    encoder_grad = jnp.einsum("rd,rl->dl", gathered, pre_grads, preferred_element_type=F32).astype(BF16)
    decoder_grad = jnp.einsum("rl,rd->ld", active, upstream, preferred_element_type=F32).astype(BF16)
    return losses[:, 0] / (every * width), encoder_grad, decoder_grad


def solution(mesh):
    n, nb = mesh.shape["shard"], mesh.shape["band"]
    return jax.shard_map(
        functools.partial(on_device, n, nb),
        mesh=mesh,
        in_specs=(
            P("shard", None),
            P(None, ("band", "shard")),
            P(("band", "shard")),
            P(("band", "shard"), None),
        ),
        out_specs=(P(), P(None, ("band", "shard")), P(("band", "shard"), None)),
        check_vma=False,
    )
```

time: 282 us -> 98.8 us (0.35)
  waiting for transfers between devices: 207 us -> 0 us
  Pallas kernels: 0 us -> 89.1 us
  blocking collectives: 21.5 us -> 0 us
  between operations: 13.8 us -> 0.64 us
  local copies, waits for them, and re-layouts: 11.9 us -> 0.01 us
  matrix products: 18.5 us -> 7.57 us
  other arithmetic: 9.06 us -> 1.3 us
    all_gather x3 -> x0, waiting for transfers between devices: 112 us -> none  [the longest x1 56.8 us: on_device(): gathered = lax.all_gather(activations, 'shard', axis=0, tiled=True)]
    reduce_scatter x1 -> x0, waiting for transfers between devices: 94.3 us -> none  [on_device(): lax.psum_scatter(jnp.dot(act_rows, decoder, preferred_element_type=jnp.fl...]
    pallas_call x0 -> x1, Pallas kernels: none -> 89.1 us  [on_device(): pl.pallas_call(functools.partial(kernel, n, nb), out_shape=(jax.ShapeDtyp...]
    psum x1 -> x0, blocking collectives: 21.5 us -> none  [on_device(): lax.psum(jnp.sum(errors_all * errors_all, axis=(1, 2)), 'shard') / divisor]
    dot_general x4 -> x2, matrix products: 18.5 us -> 7.57 us  [the longest x1 4.73 us: on_device(): jnp.einsum('rd,rl->dl', gathered, pre_grads, preferred_element_type=F32)]
    another operation x2 -> x0, other arithmetic: 6.69 us -> none  [the longest x1 3.47 us: on_device(): prefix_recon = jnp.cumsum(stacked, axis=0)]
    rev x2 -> x0, local copies, waits for them, and re-layouts: 6.68 us -> none  [on_device(): tail_sums = jnp.flip(jnp.cumsum(jnp.flip(errors_all, 0), axis=0), 0)]
    unnamed x9 -> x4, local copies, waits for them, and re-layouts: 5.27 us -> 0.01 us
  transfers between devices with their start and end apart: 4 -> 0, of which waited for: 4 -> 0; matrix products, arithmetic and copies ran while one was open for 0% -> 0% of each run, Pallas kernels for 0% -> 0%
where the time goes in v1:
time: 98.8 us; the launch traced here: 98.7 us
  Pallas kernels  89.1 us (90%)
  matrix products  7.57 us (8%)
  other arithmetic  1.3 us (1%)
    pallas_call x1, Pallas kernels, on_device(): pl.pallas_call(functools.partial(kernel, n, nb), out_shape=(jax.ShapeDtyp...  89.1 us
    dot_general x1, matrix products, on_device(): jnp.einsum('rd,rl->dl', gathered, pre_grads, preferred_element_type=F32)  4.73 us
    dot_general x1, matrix products, on_device(): jnp.einsum('rl,rd->ld', active, upstream, preferred_element_type=F32)  2.84 us

profile of v1, /device:TPU:0, one launch (start us, length us, event | category | flops | bytes accessed | tf_op | source)
XLA Modules:
  0.0 98.7 jit_solution(16800782442683891494)
XLA Ops:
  0.6 89.1 %shard_map.67 = (bf16[512,2304]{1,0:T(8,128)(2,1)}, bf16[512,2304]{1,0:T(8,128)(2,1)}, bf16[512,512]{1,0:T(8,128)(2,1)}, bf16[512,512]{1,0:T(8,128)(2,1)}, f32[4,128]{1,0:T(4,128)}) custom-call(bf16[64,2304]{1,0:T(8,128)(2,1)} %act_ref.1, bf16[4,16,2304]{2,1,0:T(8,128)(2,1)} %bitcast.6, bf16[2304,512]{1,0:T(8,128)(2,1)} %enc_hbm.1, f32[1,512]{1,0:T(1,128)} %bitcast.7, ...), custom_call_target="tpu_custom_call" | custom-call | tf_op jit(solution)/shard_map/pallas_call | solution.py:295
  89.8 1.3 %multiply_reduce_fusion = f32[4]{0:T(128)} fusion(f32[4,128]{1,0:T(4,128)} %get-tuple-element.8), kind=kLoop, calls=%fused_computation.2 | loop fusion | flops 4 | bytes 32 | tf_op jit(solution)/shard_map/div | solution.py:338
  91.1 0.0 copy-start
  91.1 0.0 copy-start.1
  91.1 4.7 %convolution_convert_fusion.1 = bf16[2304,512]{1,0:T(8,128)(2,1)} fusion(bf16[512,2304]{1,0:T(8,128)(2,1)} %get-tuple-element.9, bf16[512,512]{1,0:T(8,128)(2,1)} %get-tuple-element.10), kind=kOutput, calls=%fused_computation.1 | convolution fusion | flops 1209139200 | bytes 5242880 | tf_op jit(solution)/shard_map/rd,rl->dl/dot_general | solution.py:336
  95.8 0.0 copy-done
  95.8 0.0 copy-done.1
  95.8 2.8 %convolution_convert_fusion = bf16[512,2304]{1,0:T(8,128)(2,1)} fusion(bf16[512,512]{1,0:T(8,128)(2,1)S(1)} %copy-done.1, bf16[512,2304]{1,0:T(8,128)(2,1)S(1)} %copy-done), kind=kOutput, calls=%fused_computation | convolution fusion | flops 1209139200 | bytes 5242880 | tf_op jit(solution)/shard_map/rl,rd->ld/dot_general | solution.py:337
Async XLA Ops:
  91.1 4.7 %copy-start = (bf16[512,2304]{1,0:T(8,128)(2,1)S(1)}, bf16[512,2304]{1,0:T(8,128)(2,1)}, u32[]{:S(2)}) copy-start(bf16[512,2304]{1,0:T(8,128)(2,1)} %get-tuple-element.12) | copy-start | bytes 7077892
  91.1 4.7 %copy-start.1 = (bf16[512,512]{1,0:T(8,128)(2,1)S(1)}, bf16[512,512]{1,0:T(8,128)(2,1)}, u32[]{:S(2)}) copy-start(bf16[512,512]{1,0:T(8,128)(2,1)} %get-tuple-element.11) | copy-start | bytes 1572868

commit v2 on v0

v2 whole, which is shorter than its diff:
```python
import functools

import jax
import jax.numpy as jnp
from jax import lax
from jax.experimental import pallas as pl
from jax.experimental.pallas import tpu as pltpu
from jax.sharding import PartitionSpec as P

MESH = pl.DeviceIdType.MESH
PARTS = 2
LAG = 0
F32 = jnp.float32
BF16 = jnp.bfloat16


def factors(count):
    outer = next(a for a in range(1, count + 1) if count % a == 0 and a * a >= count)
    return outer, count // outer


def ring_position(index, outer, inner):
    z, x = index // inner, index % inner
    return x * outer + z + (x % 2) * (outer - 1 - 2 * z)


def ring_index(position, outer, inner):
    x, r = position // outer, position % outer
    z = r + (x % 2) * (outer - 1 - 2 * r)
    return z * inner + x


def tile_of(extent, most):
    return next(t for t in range(most, 0, -128) if extent % t == 0)


def kernel(
    n, nb,
    act_ref, act3_ref, enc_hbm, bias_ref, dec_hbm,
    gath_t_hbm, ups_hbm, active_hbm, pregr_hbm, loss_ref,
    gath, gath_t, ups, active, pregr,
    enc, dec, linear, part, sendb, recvb, xsend, xrecv, usend, urecv, loss_acc, loss1s, loss1, loss2s, loss2,
    load_sem, out_sem,
    ag_s, ag_r, pt_s, pt_r, rs_s, rs_r, bx_s, bx_r, bu_s, bu_r, l1_s, l1_r, l2_s, l2_r, ug_s, ug_r,
):
    width = act_ref.shape[1]
    rows = act_ref.shape[0] // PARTS
    half = rows // 2
    thin = rows // nb
    fwd, bwd = n // 2, n // 2 - 1
    outer, inner = factors(n)
    band = lax.axis_index("band")
    shard = lax.axis_index("shard")
    core = band % 2
    sign = 1 - 2 * core
    place = ring_position(shard, outer, inner)
    nxt = {"shard": ring_index((place + n + sign) % n, outer, inner)}
    prv = {"shard": ring_index((place + n - sign) % n, outer, inner)}
    mate = {"band": band + sign}

    load_enc = pltpu.make_async_copy(enc_hbm, enc, load_sem.at[0])
    load_dec = pltpu.make_async_copy(dec_hbm, dec, load_sem.at[1])
    load_enc.start()
    load_dec.start()

    barrier = pltpu.get_barrier_semaphore()
    for device in [nxt, prv] + [{"band": (band + i) % nb} for i in range(1, nb)]:
        pl.semaphore_signal(barrier, inc=1, device_id=device, device_id_type=MESH)
    pl.semaphore_wait(barrier, nb + 1)

    started = []
    written = []

    def remote(src, dst, send, recv, device):
        return pltpu.make_async_remote_copy(
            src_ref=src, dst_ref=dst, send_sem=send, recv_sem=recv, device_id=device, device_id_type=MESH
        )

    def go(copy):
        copy.start()
        started.append(copy)
        return copy

    def write(src, dst, index):
        copy = pltpu.make_async_copy(src, dst, out_sem.at[index])
        copy.start()
        written.append(copy)

    tile = tile_of(width, 768)
    step_cols = tile_of(width, 256)
    l1 = []

    def batch(m):
        base = m * n * rows

        def at(slot):
            return pl.ds(base + slot * rows, rows)

        def group_span(upper):
            return pl.ds(base + upper * fwd * rows, fwd * rows)

        def held(slot):
            start = pl.multiple_of(base + slot * rows + core * half, half)
            return gath.at[pl.ds(start, half), :]

        mine = act_ref.at[pl.ds(pl.multiple_of(m * rows + core * half, half), half), :]

        def ag_copy(way, t):
            if way == 0:
                src = mine if t == 1 else held(n - t + 1)
                return remote(src, held(n - t), ag_s.at[m, 0, t], ag_r.at[m, 0, t], nxt)
            src = mine if t == 1 else held(t - 1)
            return remote(src, held(t), ag_s.at[m, 1, t], ag_r.at[m, 1, t], prv)

        def mate_copy(slot):
            there = n - slot
            return remote(held(slot), held(there), pt_s.at[m, slot], pt_r.at[m, there], mate)

        def mate_wait(s):
            remote(held(s), held(s), pt_s.at[m, n - s], pt_r.at[m, s], mate).wait_recv()

        def preact(upper):
            span = group_span(upper)
            value = jnp.dot(gath[span, :], enc[...], preferred_element_type=F32) + bias_ref[...]
            value = jnp.maximum(value, 0.0)
            linear[span, :] = value
            active[span, :] = (value * value).astype(BF16)
            write(active.at[span, :], active_hbm.at[span, :], (0, m, upper))

        def transpose(upper):
            span = group_span(upper)
            gath_t[:, span] = gath[span, :].T
            write(gath_t.at[:, span], gath_t_hbm.at[:, span], (1, m, upper))

        def decode(upper):
            span = group_span(upper)

            def body(i, carry):
                cols = pl.ds(pl.multiple_of(i * tile, tile), tile)
                part[span, cols] = jnp.dot(active[span, :], dec[:, cols], preferred_element_type=F32)
                return carry

            lax.fori_loop(0, width // tile, body, 0)

        ag = {(0, 1): go(ag_copy(0, 1)), (1, 1): go(ag_copy(1, 1))}
        gath[at(0), :] = act_ref[pl.ds(m * rows, rows), :]
        yield
        for t in range(1, fwd + 1):
            ag[0, t].wait_recv()
            if t < fwd:
                ag[0, t + 1] = go(ag_copy(0, t + 1))
            go(mate_copy(n - t))
            if t <= bwd:
                ag[1, t].wait_recv()
                if t < bwd:
                    ag[1, t + 1] = go(ag_copy(1, t + 1))
                go(mate_copy(t))
            if t < fwd:
                yield
            if t == bwd:
                for s in range(1, fwd):
                    mate_wait(s)
                if m == 0:
                    load_enc.wait()
                preact(0)
        for s in range(fwd, n):
            mate_wait(s)
        if bwd == 0:
            if m == 0:
                load_enc.wait()
            preact(0)
        preact(1)
        if m == 0:
            load_dec.wait()
        decode(1)

        rs = {}

        def rs_copy(way, t):
            slot = fwd - t + 1 if way == 0 else fwd + t
            there = slot - 1 if way == 0 else (slot + 1 if slot + 1 < n else fwd)
            return remote(
                sendb.at[m * n + slot], recvb.at[m * n + there], rs_s.at[m, way, t], rs_r.at[m, way, t],
                nxt if way == 0 else prv,
            )

        for t in range(1, fwd + 1):
            for way in (0, 1):
                if way == 1 and t > bwd:
                    continue
                slot = fwd - t + 1 if way == 0 else fwd + t
                value = part[at(slot), :]
                if t > 1:
                    rs[way, t - 1].wait_recv()
                    value = value + recvb[m * n + slot].astype(F32)
                sendb[m * n + slot] = value.astype(BF16)
                rs[way, t] = go(rs_copy(way, t))
            yield
            if t == 1:
                decode(0)
        if bwd:
            rs[1, bwd].wait_recv()
        rs[0, fwd].wait_recv()
        value = part[at(0), :] + recvb[m * n].astype(F32)
        if bwd:
            value = value + recvb[m * n + fwd].astype(F32)
        part[at(0), :] = value
        for k in range(nb):
            xsend[m * nb + k] = part[pl.ds(base + k * thin, thin), :].astype(BF16)
        bx = [
            go(remote(
                xsend.at[m * nb + (band + i) % nb], xrecv.at[m * nb + band], bx_s.at[m, i], bx_r.at[m, i],
                {"band": (band + i) % nb},
            ))
            for i in range(1, nb)
        ]
        xrecv[m * nb + band] = xsend[m * nb + band]
        transpose(0)
        yield
        for copy in bx:
            copy.wait_recv()

        def errors(i, carry):
            cols = pl.ds(pl.multiple_of(i * step_cols, step_cols), step_cols)
            left = act3_ref[m * nb + band, :, cols].astype(F32)
            all_errors = []
            for k in range(nb):
                left = left - xrecv[m * nb + k, :, cols].astype(F32)
                all_errors.append(left)
                loss_acc[pl.ds(m * nb + k, 1), cols] = jnp.sum(left * left, axis=0, keepdims=True)
            total = jnp.zeros_like(left)
            for k in reversed(range(nb)):
                total = total + all_errors[k]
                usend[m * nb + k, :, cols] = (-total / nb).astype(BF16)
            return carry

        lax.fori_loop(0, width // step_cols, errors, 0)
        bu = [
            go(remote(
                usend.at[m * nb + (band + i) % nb], urecv.at[m * nb + band], bu_s.at[m, i], bu_r.at[m, i],
                {"band": (band + i) % nb},
            ))
            for i in range(1, nb)
        ]
        urecv[m * nb + band] = usend[m * nb + band]
        if m == PARTS - 1:
            sums = loss_acc[pl.ds(0, nb), :]
            for other in range(1, PARTS):
                sums = sums + loss_acc[pl.ds(other * nb, nb), :]
            loss1s[...] = jnp.broadcast_to(jnp.sum(sums, axis=1, keepdims=True), loss1s.shape)
            for i in range(1, nb):
                l1.append(go(remote(
                    loss1s, loss1.at[i], l1_s.at[i], l1_r.at[i], {"band": (band + i) % nb}
                )))
        transpose(1)
        yield
        for copy in bu:
            copy.wait_recv()
        ups[at(0), :] = jnp.concatenate([urecv[m * nb + k].astype(F32) for k in range(nb)], axis=0).astype(BF16)

        def ug_copy(way, t):
            if way == 0:
                slot, there, device = (n - t + 1) % n, n - t, nxt
            else:
                slot, there, device = t - 1, t, prv
            return remote(ups.at[at(slot), :], ups.at[at(there), :], ug_s.at[m, way, t], ug_r.at[m, way, t], device)

        def backward(upper):
            span = group_span(upper)
            grads = lax.dot_general(ups[span, :], dec[...], (((1,), (1,)), ((), ())), preferred_element_type=F32)
            pregr[span, :] = (2.0 * linear[span, :] * grads).astype(BF16)
            write(pregr.at[span, :], pregr_hbm.at[span, :], (3, m, upper))

        ug = {}
        for way in (0, 1):
            if way == 0 or bwd:
                ug[way, 1] = go(ug_copy(way, 1))
        yield
        for t in range(1, fwd + 1):
            for way in (0, 1):
                last = fwd if way == 0 else bwd
                if t > last:
                    continue
                ug[way, t].wait_recv()
                if t < last:
                    ug[way, t + 1] = go(ug_copy(way, t + 1))
            if t == fwd:
                write(ups.at[group_span(1), :], ups_hbm.at[group_span(1), :], (2, m, 1))
            yield
            if t == max(bwd, 1):
                write(ups.at[group_span(0), :], ups_hbm.at[group_span(0), :], (2, m, 0))
                backward(0)
        backward(1)

    work = [batch(m) for m in range(PARTS)]
    done = set()
    turn = 0
    while len(done) < PARTS:
        for m in range(PARTS):
            if m in done or turn < m * LAG:
                continue
            if next(work[m], "end") == "end":
                done.add(m)
        turn += 1
        if not len(done) and l1 and turn == n + 4 + (PARTS - 1) * LAG:
            for copy in l1:
                copy.wait_recv()
            total = loss1s[...]
            for i in range(1, nb):
                total = total + loss1[i]
            loss2s[...] = total
            l2 = [
                go(remote(loss2s, loss2.at[i], l2_s.at[i], l2_r.at[i], {"shard": (shard + i) % n}))
                for i in range(1, n)
            ]
    for copy in l2:
        copy.wait_recv()
    total = loss2s[...]
    for i in range(1, n):
        total = total + loss2[i]
    for k in range(nb):
        loss_ref[k] = jnp.sum(total[k:k + 1, 0:1]) / (n * act_ref.shape[0] * width)
    for copy in started:
        copy.wait_send()
    for copy in written:
        copy.wait()


def on_device(n, nb, activations, encoder, encoder_bias, decoder):
    local, width = activations.shape
    latents = encoder.shape[1]
    rows = local // PARTS
    every = n * local
    thin = rows // nb
    sem = pltpu.SemaphoreType.DMA
    vmem = pl.BlockSpec(memory_space=pltpu.VMEM)
    hbm = pl.BlockSpec(memory_space=pl.ANY)
    steps = n // 2 + 1
    gathered_t, upstream, active, pre_grads, losses = pl.pallas_call(
        functools.partial(kernel, n, nb),
        out_shape=(
            jax.ShapeDtypeStruct((width, every), BF16),
            jax.ShapeDtypeStruct((every, width), BF16),
            jax.ShapeDtypeStruct((every, latents), BF16),
            jax.ShapeDtypeStruct((every, latents), BF16),
            jax.ShapeDtypeStruct((nb,), F32),
        ),
        in_specs=[vmem, vmem, hbm, vmem, hbm],
        out_specs=[hbm] * 4 + [pl.BlockSpec(memory_space=pltpu.SMEM)],
        scratch_shapes=[
            pltpu.VMEM((every, width), BF16),
            pltpu.VMEM((width, every), BF16),
            pltpu.VMEM((every, width), BF16),
            pltpu.VMEM((every, latents), BF16),
            pltpu.VMEM((every, latents), BF16),
            pltpu.VMEM((width, latents), BF16),
            pltpu.VMEM((latents, width), BF16),
            pltpu.VMEM((every, latents), F32),
            pltpu.VMEM((every, width), F32),
            pltpu.VMEM((PARTS * n, rows, width), BF16),
            pltpu.VMEM((PARTS * n, rows, width), BF16),
            pltpu.VMEM((PARTS * nb, thin, width), BF16),
            pltpu.VMEM((PARTS * nb, thin, width), BF16),
            pltpu.VMEM((PARTS * nb, thin, width), BF16),
            pltpu.VMEM((PARTS * nb, thin, width), BF16),
            pltpu.VMEM((PARTS * nb, width), F32),
            pltpu.VMEM((nb, 128), F32),
            pltpu.VMEM((nb, nb, 128), F32),
            pltpu.VMEM((nb, 128), F32),
            pltpu.VMEM((n, nb, 128), F32),
            sem((2,)), sem((4, PARTS, 2)),
            sem((PARTS, 2, steps)), sem((PARTS, 2, steps)),
            sem((PARTS, n)), sem((PARTS, n)),
            sem((PARTS, 2, steps)), sem((PARTS, 2, steps)),
            sem((PARTS, nb)), sem((PARTS, nb)),
            sem((PARTS, nb)), sem((PARTS, nb)),
            sem((nb,)), sem((nb,)),
            sem((n,)), sem((n,)),
            sem((PARTS, 2, steps)), sem((PARTS, 2, steps)),
        ],
        compiler_params=pltpu.CompilerParams(
            collective_id=0, has_side_effects=True, vmem_limit_bytes=60 * 1024 * 1024
        ),
    )(activations, activations.reshape(PARTS * nb, thin, width), encoder, encoder_bias.reshape(1, latents), decoder)
    encoder_grad = jnp.einsum("dr,rl->dl", gathered_t, pre_grads, preferred_element_type=F32).astype(BF16)
    decoder_grad = jnp.einsum("rl,rd->ld", active, upstream, preferred_element_type=F32).astype(BF16)
    return losses, encoder_grad, decoder_grad


def solution(mesh):
    n, nb = mesh.shape["shard"], mesh.shape["band"]
    return jax.shard_map(
        functools.partial(on_device, n, nb),
        mesh=mesh,
        in_specs=(
            P("shard", None),
            P(None, ("band", "shard")),
            P(("band", "shard")),
            P(("band", "shard"), None),
        ),
        out_specs=(P(), P(None, ("band", "shard")), P(("band", "shard"), None)),
        check_vma=False,
    )
```

time: 282 us -> 90.8 us (0.32)
  waiting for transfers between devices: 207 us -> 0 us
  Pallas kernels: 0 us -> 81.9 us
  blocking collectives: 21.5 us -> 0 us
  between operations: 13.8 us -> 0.66 us
  local copies, waits for them, and re-layouts: 11.9 us -> 0.52 us
  matrix products: 18.5 us -> 7.53 us
  other arithmetic: 9.06 us -> 0 us
    all_gather x3 -> x0, waiting for transfers between devices: 112 us -> none  [the longest x1 56.8 us: on_device(): gathered = lax.all_gather(activations, 'shard', axis=0, tiled=True)]
    reduce_scatter x1 -> x0, waiting for transfers between devices: 94.3 us -> none  [on_device(): lax.psum_scatter(jnp.dot(act_rows, decoder, preferred_element_type=jnp.fl...]
    pallas_call x0 -> x1, Pallas kernels: none -> 81.9 us  [on_device(): pl.pallas_call(functools.partial(kernel, n, nb), out_shape=(jax.ShapeDtyp...]
    psum x1 -> x0, blocking collectives: 21.5 us -> none  [on_device(): lax.psum(jnp.sum(errors_all * errors_all, axis=(1, 2)), 'shard') / divisor]
    dot_general x4 -> x2, matrix products: 18.5 us -> 7.53 us  [the longest x1 4.69 us: on_device(): jnp.einsum('dr,rl->dl', gathered_t, pre_grads, preferred_element_type=F32)]
    another operation x2 -> x0, other arithmetic: 6.69 us -> none  [the longest x1 3.47 us: on_device(): prefix_recon = jnp.cumsum(stacked, axis=0)]
    rev x2 -> x0, local copies, waits for them, and re-layouts: 6.68 us -> none  [on_device(): tail_sums = jnp.flip(jnp.cumsum(jnp.flip(errors_all, 0), axis=0), 0)]
    unnamed x9 -> x7, local copies, waits for them, and re-layouts: 5.27 us -> 0.52 us
  transfers between devices with their start and end apart: 4 -> 0, of which waited for: 4 -> 0; matrix products, arithmetic and copies ran while one was open for 0% -> 0% of each run, Pallas kernels for 0% -> 0%
where the time goes in v2:
time: 90.8 us; the launch traced here: 90.6 us
  Pallas kernels  81.9 us (90%)
  matrix products  7.53 us (8%)
    pallas_call x1, Pallas kernels, on_device(): pl.pallas_call(functools.partial(kernel, n, nb), out_shape=(jax.ShapeDtyp...  81.9 us
    dot_general x1, matrix products, on_device(): jnp.einsum('dr,rl->dl', gathered_t, pre_grads, preferred_element_type=F32)  4.69 us
    dot_general x1, matrix products, on_device(): jnp.einsum('rl,rd->ld', active, upstream, preferred_element_type=F32)  2.84 us

profile of v2, /device:TPU:0, one launch (start us, length us, event | category | flops | bytes accessed | tf_op | source)
XLA Modules:
  0.0 90.6 jit_solution(373219523535668318)
XLA Ops:
  0.6 81.9 %shard_map.67 = (bf16[2304,512]{1,0:T(8,128)(2,1)}, bf16[512,2304]{1,0:T(8,128)(2,1)}, bf16[512,512]{1,0:T(8,128)(2,1)}, bf16[512,512]{1,0:T(8,128)(2,1)}, f32[4]{0:T(128)}) custom-call(bf16[64,2304]{1,0:T(8,128)(2,1)} %act_ref.1, bf16[8,8,2304]{2,1,0:T(8,128)(2,1)} %bitcast.6, bf16[2304,512]{1,0:T(8,128)(2,1)} %enc_hbm.1, f32[1,512]{1,0:T(1,128)} %bitcast.7, ...), custom_call_target="tpu_custom_call" | custom-call | tf_op jit(solution)/shard_map/pallas_call | solution.py:339
  82.5 0.0 copy-start
  82.5 0.0 copy-start.1
  82.5 4.7 %convolution_convert_fusion.1 = bf16[2304,512]{1,0:T(8,128)(2,1)} fusion(bf16[2304,512]{1,0:T(8,128)(2,1)} %get-tuple-element.9, bf16[512,512]{1,0:T(8,128)(2,1)} %get-tuple-element.10), kind=kOutput, calls=%fused_computation.1 | convolution fusion | flops 1209139200 | bytes 5242880 | tf_op jit(solution)/shard_map/dr,rl->dl/dot_general | solution.py:385
  87.2 0.0 copy-done
  87.2 0.0 copy-done.1
  87.2 0.0 copy-start.2
  87.2 2.8 %convolution_convert_fusion = bf16[512,2304]{1,0:T(8,128)(2,1)} fusion(bf16[512,512]{1,0:T(8,128)(2,1)S(1)} %copy-done.1, bf16[512,2304]{1,0:T(8,128)(2,1)S(1)} %copy-done), kind=kOutput, calls=%fused_computation | convolution fusion | flops 1209139200 | bytes 5242880 | tf_op jit(solution)/shard_map/rl,rd->ld/dot_general | solution.py:386
  90.1 0.0 copy-done.2
  90.1 0.5 copy.8
Async XLA Ops:
  82.5 4.7 %copy-start = (bf16[512,2304]{1,0:T(8,128)(2,1)S(1)}, bf16[512,2304]{1,0:T(8,128)(2,1)}, u32[]{:S(2)}) copy-start(bf16[512,2304]{1,0:T(8,128)(2,1)} %get-tuple-element.12) | copy-start | bytes 7077892
  82.5 4.7 %copy-start.1 = (bf16[512,512]{1,0:T(8,128)(2,1)S(1)}, bf16[512,512]{1,0:T(8,128)(2,1)}, u32[]{:S(2)}) copy-start(bf16[512,512]{1,0:T(8,128)(2,1)} %get-tuple-element.11) | copy-start | bytes 1572868
  87.2 2.9 %copy-start.2 = (f32[4]{0:T(128)S(1)}, f32[4]{0:T(128)}, u32[]{:S(2)}) copy-start(f32[4]{0:T(128)} %get-tuple-element.16) | copy-start | bytes 52

commit v3 on v2

--- a/solution.py
+++ b/solution.py
@@ -382,8 +382,32 @@
             collective_id=0, has_side_effects=True, vmem_limit_bytes=60 * 1024 * 1024
         ),
     )(activations, activations.reshape(PARTS * nb, thin, width), encoder, encoder_bias.reshape(1, latents), decoder)
-    encoder_grad = jnp.einsum("dr,rl->dl", gathered_t, pre_grads, preferred_element_type=F32).astype(BF16)
-    decoder_grad = jnp.einsum("rl,rd->ld", active, upstream, preferred_element_type=F32).astype(BF16)
+    def grads(e_ref, f_ref, g_ref, h_ref, eo_ref, do_ref):
+        eo_ref[...] = jnp.dot(e_ref[...], f_ref[...], preferred_element_type=F32).astype(BF16)
+        do_ref[...] = lax.dot_general(
+            g_ref[...], h_ref[...], (((0,), (0,)), ((), ())), preferred_element_type=F32
+        ).astype(BF16)
+
+    wide = tile_of(width, 1152)
+    encoder_grad, decoder_grad = pl.pallas_call(
+        grads,
+        grid=(width // wide,),
+        out_shape=(
+            jax.ShapeDtypeStruct((width, latents), BF16),
+            jax.ShapeDtypeStruct((latents, width), BF16),
+        ),
+        in_specs=[
+            pl.BlockSpec((wide, every), lambda i: (i, 0)),
+            pl.BlockSpec((every, latents), lambda i: (0, 0)),
+            pl.BlockSpec((every, latents), lambda i: (0, 0)),
+            pl.BlockSpec((every, wide), lambda i: (0, i)),
+        ],
+        out_specs=[
+            pl.BlockSpec((wide, latents), lambda i: (i, 0)),
+            pl.BlockSpec((latents, wide), lambda i: (0, i)),
+        ],
+        compiler_params=pltpu.CompilerParams(vmem_limit_bytes=60 * 1024 * 1024),
+    )(gathered_t, pre_grads, active, upstream)
     return losses, encoder_grad, decoder_grad
 
 

time: 90.8 us -> 89.2 us (0.982)
  matrix products: 7.53 us -> 0 us
  Pallas kernels: 81.9 us -> 87.8 us
    dot_general x2 -> x0, matrix products: 7.53 us -> none  [the longest x1 4.69 us: on_device(): jnp.einsum('dr,rl->dl', gathered_t, pre_grads, preferred_element_type=F32)]
    pallas_call x0 -> x1, Pallas kernels: none -> 5.9 us  [on_device(): pl.pallas_call(grads, grid=(width // wide,), out_shape=(jax.ShapeDtypeStr...]
where the time goes in v3:
time: 89.2 us; the launch traced here: 89 us
  Pallas kernels  87.8 us (98%)
    pallas_call x1, Pallas kernels, on_device(): pl.pallas_call(functools.partial(kernel, n, nb), out_shape=(jax.ShapeDtyp...  81.9 us
    pallas_call x1, Pallas kernels, on_device(): pl.pallas_call(grads, grid=(width // wide,), out_shape=(jax.ShapeDtypeStr...  5.9 us

profile of v3, /device:TPU:0, one launch (start us, length us, event | category | flops | bytes accessed | tf_op | source)
XLA Modules:
  0.0 89.0 jit_solution(1383324829717524742)
XLA Ops:
  0.6 81.9 %shard_map.67 = (bf16[2304,512]{1,0:T(8,128)(2,1)}, bf16[512,2304]{1,0:T(8,128)(2,1)}, bf16[512,512]{1,0:T(8,128)(2,1)}, bf16[512,512]{1,0:T(8,128)(2,1)}, f32[4]{0:T(128)}) custom-call(bf16[64,2304]{1,0:T(8,128)(2,1)} %act_ref.1, bf16[8,8,2304]{2,1,0:T(8,128)(2,1)} %bitcast.2, bf16[2304,512]{1,0:T(8,128)(2,1)} %enc_hbm.1, f32[1,512]{1,0:T(1,128)} %bitcast.3, ...), custom_call_target="tpu_custom_call" | custom-call | tf_op jit(solution)/shard_map/pallas_call | solution.py:339
  82.5 0.0 copy-start
  82.6 5.9 %shard_map.68 = (bf16[2304,512]{1,0:T(8,128)(2,1)}, bf16[512,2304]{1,0:T(8,128)(2,1)}) custom-call(bf16[2304,512]{1,0:T(8,128)(2,1)} %get-tuple-element.11.e_ref, bf16[512,512]{1,0:T(8,128)(2,1)} %get-tuple-element.12.f_ref, bf16[512,512]{1,0:T(8,128)(2,1)} %get-tuple-element.13.g_ref, bf16[512,2304]{1,0:T(8,128)(2,1)} %get-tuple-element.14.h_ref), custom_call_target="tpu_custom_call" | custom-call | tf_op jit(solution)/shard_map/pallas_call | solution.py:392
  88.5 0.0 copy-done
  88.5 0.5 copy.8
Async XLA Ops:
  82.5 5.9 %copy-start = (f32[4]{0:T(128)S(1)}, f32[4]{0:T(128)}, u32[]{:S(2)}) copy-start(f32[4]{0:T(128)} %get-tuple-element.20) | copy-start | bytes 52
